TPU v7x, 512 devices: a whole 4x4x16 slice. The times are simulated.
512 devices in a mesh: fsdp: 16 (over x, y_lo, core), tm: 32 (over y_hi, z).
Axes of the slice: x: 4, y: 4 (y_hi: 2, y_lo: 2; y = y_hi * 2 + y_lo), z: 16, core: 2. Of those that a mesh axis runs over, the one named last changes fastest.
Arguments:
- tokens: bfloat16 [32, 32, 256, 1024], P('fsdp', 'tm'), may hold values from -6 to 6
- spatial_gain: float32 [1024], replicated, may hold values from 0.25 to 1.75
- spatial_qkv: bfloat16 [1024, 1536], P('fsdp'), may hold values from -16 to 16
- spatial_out: bfloat16 [512, 1024], P('fsdp'), may hold values from -0.25 to 0.25
- temporal_gain: float32 [1024], replicated, may hold values from 0.25 to 1.75
- temporal_qkv: bfloat16 [1024, 1536], P('fsdp'), may hold values from -16 to 16
- temporal_out: bfloat16 [512, 1024], P('fsdp'), may hold values from -0.25 to 0.25
Outputs:
- encoded: bfloat16 [32, 32, 256, 1024], P('fsdp', 'tm')
All inputs are finite; a program needn't handle non-finite values.
Results may differ from a plain program's by a relative error of at most 0.0061.
Values may be sent and summed in bfloat16 or wider, within the bound.
No kernel may reach another device: no remote copies, remote signals or barrier semaphores. Data moves between devices by JAX's collectives and lax.ppermute only.
A program may use at most 64 MiB of HBM per device.

v0:
```python
import jax
import jax.numpy as jnp
from jax import lax
from jax.sharding import PartitionSpec as P

HEAD = 64
HEADS = 8
INNER = 512
EPSILON = 1e-06


def laid_out(pieces, dim):
    pieces = jnp.moveaxis(pieces, 0, dim)
    shape = pieces.shape
    return pieces.reshape(*shape[:dim], shape[dim] * shape[dim + 1], *shape[dim + 2 :])


def sent_to_all(shard, axis):
    copies = jnp.broadcast_to(shard, (lax.axis_size(axis), *shard.shape))
    return lax.all_to_all(copies, axis, split_axis=0, concat_axis=0, tiled=True)


def gathered_copies(shard, axis, dim):
    return laid_out(sent_to_all(shard, axis), dim)


def norm_rows(source, norm_gain):
    values = source.astype(jnp.float32)
    centre = values - jnp.mean(values, axis=-1, keepdims=True)
    spread = jnp.mean(centre * centre, axis=-1, keepdims=True)
    return (centre * lax.rsqrt(spread + EPSILON) * norm_gain).astype(jnp.bfloat16)


def attention_core(projected):
    inner_width = projected.shape[-1] // 3
    lead_shape = projected.shape[:-1]
    queries = projected[..., :inner_width].reshape(lead_shape + (HEADS, HEAD))
    key_rows = projected[..., inner_width : 2 * inner_width].reshape(lead_shape + (HEADS, HEAD))
    value_rows = (
        projected[..., 2 * inner_width :].astype(jnp.bfloat16).reshape(lead_shape + (HEADS, HEAD))
    )
    scores = jnp.einsum("blmhe,bkmhe->bmhlk", queries, key_rows) * HEAD ** (-0.5)
    row_max = jnp.max(scores, axis=-1, keepdims=True)
    exponent = jnp.exp(scores - row_max)
    weights = (exponent / jnp.sum(exponent, axis=-1, keepdims=True)).astype(jnp.bfloat16)
    context = jnp.einsum(
        "bmhlk,bkmhe->blmhe", weights, value_rows, preferred_element_type=jnp.float32
    )
    return context.astype(jnp.bfloat16).reshape(lead_shape + (inner_width,))


def project_inputs(normed, weight):

    def add_rows(running, segment, offset):
        return jnp.dot(normed, segment, preferred_element_type=jnp.float32)

    initial = jnp.zeros((normed.shape[0], weight.shape[1]), jnp.float32)
    return add_rows(initial, lax.all_gather(weight, "fsdp", axis=0, tiled=True), jnp.int32(0))


def project_outputs(context, weight):

    def add_rows(running, segment, offset):
        return jnp.dot(context, segment, preferred_element_type=jnp.float32)

    initial = jnp.zeros((context.shape[0], weight.shape[1]), jnp.float32)
    return add_rows(initial, gathered_copies(weight, "fsdp", 0), jnp.int32(0))


def shards(
    tokens, spatial_gain, spatial_qkv, spatial_out, temporal_gain, temporal_qkv, temporal_out
):
    clip_count, frames, places, feature_width = tokens.shape
    row_count = clip_count * frames * places
    normed = norm_rows(tokens, spatial_gain).reshape(row_count, feature_width)
    projected = project_inputs(normed, spatial_qkv).reshape(
        clip_count * frames, places, 1, 3 * INNER
    )
    context = attention_core(projected).reshape(row_count, INNER)
    middle = (
        tokens.reshape(row_count, feature_width).astype(jnp.float32)
        + project_outputs(context, spatial_out)
    ).astype(jnp.bfloat16)
    middle = middle.reshape(clip_count, frames, places, feature_width)
    arrived = lax.all_to_all(middle, "tm", split_axis=2, concat_axis=1, tiled=True)
    full_frames = arrived.shape[1]
    few_places = arrived.shape[2]
    normed_t = norm_rows(arrived, temporal_gain).reshape(row_count, feature_width)
    projected_t = project_inputs(normed_t, temporal_qkv).reshape(
        clip_count, full_frames, few_places, 3 * INNER
    )
    context_t = attention_core(projected_t)
    returned_ctx = lax.all_to_all(context_t, "tm", split_axis=1, concat_axis=2, tiled=True)
    finished = middle.reshape(row_count, feature_width).astype(jnp.float32) + project_outputs(
        returned_ctx.reshape(row_count, INNER), temporal_out
    )
    return finished.astype(jnp.bfloat16).reshape(clip_count, frames, places, feature_width)


def solution(mesh):
    placed = (
        P("fsdp", "tm", None, None),
        P(),
        P("fsdp", None),
        P("fsdp", None),
        P(),
        P("fsdp", None),
        P("fsdp", None),
    )
    return jax.shard_map(
        shards, mesh=mesh, in_specs=placed, out_specs=P("fsdp", "tm", None, None), check_vma=False
    )
```

profile of v0, /device:TPU:32, one launch (start us, length us, event | category | flops | bytes accessed | tf_op | source)
XLA Modules:
  0.0 228.6 jit_solution(6030307744431917893)
XLA Ops:
  6.5 0.7 all-gather.3.cloned.1.call-update
  7.3 1.9 broadcast_in_dim.4
  9.2 5.6 %all-to-all-start = ((bf16[16,32,1024]{2,1,0:T(8,128)(2,1)}), bf16[16,32,1024]{2,1,0:T(8,128)(2,1)}, u32[]{:S(2)}, u32[]{:S(2)}) async-start(bf16[16,32,1024]{2,1,0:T(8,128)(2,1)} %broadcast_in_dim.4), calls=%async_computation | async-start | bytes 2097152 | tf_op jit(solution)/shard_map/all_to_all | solution.py:20
  14.9 0.7 all-gather.5.cloned.1.call-update
  15.6 0.2 convert_reduce_fusion
  15.8 0.4 multiply_reduce_fusion.2
  16.2 40.8 %all-gather.3.cloned.1.call-done = bf16[1024,1536]{1,0:T(8,128)(2,1)} async-done(((bf16[64,1536]{1,0:T(8,128)(2,1)}), bf16[1024,1536]{1,0:T(8,128)(2,1)}) %all-gather.3.cloned.1.call-update) | async-done | bytes 3145744 | tf_op jit(solution)/shard_map/all_gather | solution.py:58
  57.0 3.8 %convolution_bitcast_fusion = bf16[2,256,1,1536]{3,1,0,2:T(8,128)(2,1)S(1)} fusion(bf16[1024,1536]{1,0:T(8,128)(2,1)} %all-gather.3.cloned.1.call-done, bf16[2,1,256,1024]{3,2,1,0:T(8,128)(2,1)S(1)} %copy-done, f32[1024]{0:T(1024)S(1)} %copy-done.4, f32[2,256]{1,0:T(2,128)S(1)} %add_rsqrt_fusion.1, f32[2,256]{1,0:T(2,128)S(1)} %broadcast_multiply_fusion.1), kind=kOutput, calls=%fused_computation.6 | convolution fusion | flops 1613234176 | bytes 5775360 | tf_op jit(solution)/shard_map/dot_general | solution.py:55
  61.6 3.5 %fusion.39 = (f32[2,8,256]{2,1,0:T(8,128)S(1)}, f32[2,8,256,256]{2,3,1,0:T(8,128)}) fusion(bf16[2,256,8,64]{1,3,2,0:T(8,128)(2,1)S(1)} %bitcast.67, bf16[2,256,8,64]{1,3,2,0:T(8,128)(2,1)S(1)} %bitcast.69), kind=kOutput, calls=%fused_computation.56 | convolution fusion | flops 137363712 | bytes 5259264 | tf_op jit(solution)/shard_map/sub | solution.py:44
  65.0 2.7 %fusion.20 = bf16[2,256,1,8,64]{1,4,3,0,2:T(8,128)(2,1)S(1)} fusion(bf16[2,256,8,64]{1,3,2,0:T(8,128)(2,1)S(1)} %bitcast.70, f32[2,8,256,256]{2,3,1,0:T(8,128)} %get-tuple-element.12, f32[2,8,256]{2,1,0:T(8,128)S(1)} %get-tuple-element.11), kind=kOutput, calls=%fused_computation.33 | convolution fusion | flops 136577024 | bytes 5259264 | tf_op jit(solution)/shard_map/bmhlk,bkmhe->blmhe/dot_general | solution.py:46
  67.7 0.5 copy.82
  68.4 2.0 fusion.8
  70.3 1.1 copy.83
  71.4 71.4 %all_to_all.28 = bf16[2,1,256,1024]{3,0,1,2:T(2,128)(2,1)S(1)} all-to-all(bf16[2,1,256,1024]{3,0,1,2:T(2,128)(2,1)S(1)} %copy.83), channel_id=1, replica_groups=mesh['fsdp'=16,'tm'=32] {'tm'}, dimensions={2} | all-to-all | bytes 2097152 | tf_op jit(solution)/shard_map/all_to_all | solution.py:85
  142.9 0.9 convert_reduce_fusion.1
  143.8 1.8 multiply_reduce_fusion.1
  145.6 0.3 copy.118
  145.9 0.3 copy.119
  146.2 0.9 convert.12
  147.1 4.0 %fusion.5 = bf16[2,32,8,1536]{3,2,1,0:T(8,128)(2,1)S(1)} fusion(bf16[1024,1536]{1,0:T(8,128)(2,1)} %all-gather.5.cloned.1.call-done, f32[2,32,8,1024]{3,0,2,1:T(2,128)S(1)} %convert.12, f32[1024]{0:T(1024)S(1)} %copy-done.5, f32[2,32,8]{2,1,0:T(8,128)S(1)} %copy.118, f32[2,32,8]{2,1,0:T(8,128)S(1)} %copy.119), kind=kOutput, calls=%fused_computation.7 | convolution fusion | flops 1612709888 | bytes 6823936 | tf_op jit(solution)/shard_map/dot_general | solution.py:55
  151.3 0.5 reshape.163
  151.8 0.5 reshape.164
  152.3 1.5 reshape.162
  153.9 3.2 %fusion.40 = (f32[2,8,8,32]{3,2,1,0:T(8,128)S(1)}, f32[2,8,8,32,32]{3,4,2,1,0:T(8,128)}) fusion(bf16[2,32,8,8,64]{4,3,2,1,0:T(8,128)(2,1)S(1)} %reshape.164, bf16[2,32,8,8,64]{4,3,2,1,0:T(8,128)(2,1)S(1)} %reshape.163), kind=kOutput, calls=%fused_computation.57 | convolution fusion | flops 17170464 | bytes 1589248 | tf_op jit(solution)/shard_map/sub | solution.py:44
  157.1 2.9 %fusion.18 = bf16[2,32,8,8,64]{4,1,3,2,0:T(8,128)(2,1)S(1)} fusion(f32[2,8,8,32,32]{3,4,2,1,0:T(8,128)} %get-tuple-element.14, bf16[2,32,8,8,64]{4,3,2,1,0:T(8,128)(2,1)} %reshape.162, f32[2,8,8,32]{3,2,1,0:T(8,128)S(1)} %get-tuple-element.13), kind=kOutput, calls=%fused_computation.31 | convolution fusion | flops 17301504 | bytes 1589248 | tf_op jit(solution)/shard_map/bmhlk,bkmhe->blmhe/dot_general | solution.py:46
  159.9 0.4 copy.99
  160.3 0.6 reshape.173
  161.0 37.9 %all_to_all.29 = bf16[2,32,8,512]{3,2,0,1:T(8,128)(2,1)S(1)} all-to-all(bf16[2,32,8,512]{3,2,0,1:T(8,128)(2,1)S(1)} %reshape.173), channel_id=1, replica_groups=mesh['fsdp'=16,'tm'=32] {'tm'}, dimensions={1} | all-to-all | bytes 1048576 | tf_op jit(solution)/shard_map/all_to_all | solution.py:93
  198.8 1.1 broadcast_in_dim.5
  199.9 3.7 %all-to-all-start.3 = ((bf16[16,32,1024]{2,1,0:T(8,128)(2,1)}), bf16[16,32,1024]{2,1,0:T(8,128)(2,1)S(1)}, u32[]{:S(2)}, u32[]{:S(2)}) async-start(bf16[16,32,1024]{2,1,0:T(8,128)(2,1)} %broadcast_in_dim.5), calls=%async_computation.3 | async-start | bytes 2097152 | tf_op jit(solution)/shard_map/all_to_all | solution.py:20
  203.7 16.4 %all-to-all-done.3 = bf16[16,32,1024]{2,1,0:T(8,128)(2,1)S(1)} async-done(((bf16[16,32,1024]{2,1,0:T(8,128)(2,1)}), bf16[16,32,1024]{2,1,0:T(8,128)(2,1)S(1)}, u32[]{:S(2)}, u32[]{:S(2)}) %all-to-all-start.3) | async-done | bytes 1048608 | tf_op jit(solution)/shard_map/all_to_all | solution.py:20
  220.1 1.7 add_convert_fusion
  (28 shorter events, 1.2 us)
Async XLA Ops:
  6.5 9.0 %copy-start = (bf16[2,1,256,1024]{3,2,1,0:T(8,128)(2,1)S(1)}, bf16[2,1,256,1024]{3,2,1,0:T(8,128)(2,1)}, u32[]{:S(2)}) copy-start(bf16[2,1,256,1024]{3,2,1,0:T(8,128)(2,1)} %param.7) | copy-start | bytes 3145732
  6.5 50.5 %all-gather.3.cloned.1.call-start = ((), (), s32[]{:S(2)}) async-start(), calls=%async_computation.4 | async-start | bytes 3342336 | tf_op jit(solution)/shard_map/all_gather | solution.py:58
  9.2 47.8 %copy-start.4 = (f32[1024]{0:T(1024)S(1)}, f32[1024]{0:T(1024)}, u32[]{:S(2)}) copy-start(f32[1024]{0:T(1024)} %param.8) | copy-start | bytes 12292
  9.2 59.2 %all-to-all-start = ((bf16[16,32,1024]{2,1,0:T(8,128)(2,1)}), bf16[16,32,1024]{2,1,0:T(8,128)(2,1)}, u32[]{:S(2)}, u32[]{:S(2)}) async-start(bf16[16,32,1024]{2,1,0:T(8,128)(2,1)} %broadcast_in_dim.4), calls=%async_computation | async-start | bytes 2097152 | tf_op jit(solution)/shard_map/all_to_all | solution.py:20
  14.8 132.3 %all-gather.5.cloned.1.call-start = ((), (), s32[]{:S(2)}) async-start(), calls=%async_computation.5 | async-start | bytes 3342336 | tf_op jit(solution)/shard_map/all_gather | solution.py:58
  70.3 72.5 %copy-start.1 = (bf16[512,1024]{1,0:T(8,128)(2,1)}, bf16[512,1024]{1,0:T(8,128)(2,1)S(1)}, u32[]{:S(2)}) copy-start(bf16[512,1024]{1,0:T(8,128)(2,1)S(1)} %fusion.8) | copy-start | bytes 3145732
  145.6 1.5 copy-start.5
  159.9 38.9 %copy-start.3 = (bf16[32,1024]{1,0:T(8,128)(2,1)S(1)}, bf16[32,1024]{1,0:T(8,128)(2,1)}, u32[]{:S(2)}) copy-start(bf16[32,1024]{1,0:T(8,128)(2,1)} %param.13) | copy-start | bytes 196612
  198.8 21.2 %copy-start.2 = (bf16[512,1024]{1,0:T(8,128)(2,1)S(1)}, bf16[512,1024]{1,0:T(8,128)(2,1)}, u32[]{:S(2)}) copy-start(bf16[512,1024]{1,0:T(8,128)(2,1)} %copy-done.1) | copy-start | bytes 3145732
  199.9 20.1 %all-to-all-start.3 = ((bf16[16,32,1024]{2,1,0:T(8,128)(2,1)}), bf16[16,32,1024]{2,1,0:T(8,128)(2,1)S(1)}, u32[]{:S(2)}, u32[]{:S(2)}) async-start(bf16[16,32,1024]{2,1,0:T(8,128)(2,1)} %broadcast_in_dim.5), calls=%async_computation.3 | async-start | bytes 2097152 | tf_op jit(solution)/shard_map/all_to_all | solution.py:20
Sparse Core Ops, SparseCore 0:
  9.5 47.4 all-gather.2
  59.1 44.3 all-gather.4
where the time goes:
time: 229 us
  blocking collectives  109 us (48%)
  waiting for transfers between devices  58.6 us (26%)
  matrix products  23.6 us (10%)
  between operations  13.6 us (6%)
  local copies, waits for them, and re-layouts  9.84 us (4%)
  starting transfers between devices  9.3 us (4%)
  other arithmetic  4.31 us (2%)
    all_to_all x1, blocking collectives, shards(): lax.all_to_all(middle, 'tm', split_axis=2, concat_axis=1, tiled=True)  71.4 us
    all_gather x2, waiting for transfers between devices, project_inputs(): lax.all_gather(weight, 'fsdp', axis=0, tiled=True)  40.8 us
    all_to_all x1, blocking collectives, shards(): lax.all_to_all(context_t, 'tm', split_axis=1, concat_axis=2, tiled=True)  37.9 us
    all_to_all x2, waiting for transfers between devices, sent_to_all(): return lax.all_to_all(copies, axis, split_axis=0, concat_axis=0, tiled=True)  16.4 us
    all_to_all x2, starting transfers between devices, sent_to_all(): return lax.all_to_all(copies, axis, split_axis=0, concat_axis=0, tiled=True)  9.25 us
    dot_general x2, matrix products, add_rows(): return jnp.dot(normed, segment, preferred_element_type=jnp.float32)  7.8 us
    sub x2, matrix products, attention_core(): exponent = jnp.exp(scores - row_max)  6.63 us
    dot_general x2, matrix products, attention_core(): jnp.einsum('bmhlk,bkmhe->blmhe', weights, value_rows, preferred_element_t...  5.53 us
  transfers between devices with their start and end apart: 4, of which 2 were waited for; matrix products, arithmetic and copies ran while one was open for 9% of the time, Pallas kernels for 0%

commit v1 on v0

--- a/solution.py
+++ b/solution.py
@@ -55,7 +55,13 @@
         return jnp.dot(normed, segment, preferred_element_type=jnp.float32)
 
     initial = jnp.zeros((normed.shape[0], weight.shape[1]), jnp.float32)
-    return add_rows(initial, lax.all_gather(weight, "fsdp", axis=0, tiled=True), jnp.int32(0))
+    return add_rows(
+        initial,
+        jnp.concatenate(
+            lax.all_to_all(jnp.stack([weight] * lax.axis_size("fsdp")), "fsdp", 0, 0), axis=0
+        ),
+        jnp.int32(0),
+    )
 
 
 def project_outputs(context, weight):

time: 229 us -> 277 us (1.21)
  waiting for transfers between devices: 58.6 us -> 94.7 us
  starting transfers between devices: 9.3 us -> 26.7 us
  between operations: 13.6 us -> 0.25 us
  local copies, waits for them, and re-layouts: 9.84 us -> 14.4 us
  blocking collectives: 109 us -> 112 us
    all_to_all x0 -> x2, waiting for transfers between devices: none -> 73.1 us  [project_inputs(): lax.all_to_all(jnp.stack([weight] * lax.axis_size('fsdp')), 'fsdp', 0, 0)]
    all_gather x2 -> x0, waiting for transfers between devices: 40.8 us -> none  [project_inputs(): lax.all_gather(weight, 'fsdp', axis=0, tiled=True)]
    all_to_all x0 -> x2, starting transfers between devices: none -> 10.3 us  [project_inputs(): lax.all_to_all(jnp.stack([weight] * lax.axis_size('fsdp')), 'fsdp', 0, 0)]
    all_to_all x2, starting transfers between devices: 9.25 us -> 16.4 us  [sent_to_all(): return lax.all_to_all(copies, axis, split_axis=0, concat_axis=0, tiled=True)]
    all_to_all x2, waiting for transfers between devices: 16.4 us -> 21.6 us  [sent_to_all(): return lax.all_to_all(copies, axis, split_axis=0, concat_axis=0, tiled=True)]
    another operation x0 -> x2, local copies, waits for them, and re-layouts: none -> 4.94 us  [project_inputs(): jnp.stack([weight] * lax.axis_size('fsdp'))]
  transfers between devices with their start and end apart: 4 -> 4, of which waited for: 2 -> 4; matrix products, arithmetic and copies ran while one was open for 9% -> 6% of each run, Pallas kernels for 0% -> 0%
where the time goes in v1:
time: 277 us; the launch traced here: 276 us
  blocking collectives  112 us (40%)
  waiting for transfers between devices  94.7 us (34%)
  starting transfers between devices  26.7 us (10%)
  matrix products  23.3 us (8%)
  local copies, waits for them, and re-layouts  14.4 us (5%)
  other arithmetic  4.94 us (2%)
    all_to_all x1, blocking collectives, shards(): lax.all_to_all(middle, 'tm', split_axis=2, concat_axis=1, tiled=True)  73.4 us
    all_to_all x2, waiting for transfers between devices, project_inputs(): lax.all_to_all(jnp.stack([weight] * lax.axis_size('fsdp')), 'fsdp', 0, 0)  73.1 us
    all_to_all x1, blocking collectives, shards(): lax.all_to_all(context_t, 'tm', split_axis=1, concat_axis=2, tiled=True)  38.4 us
    all_to_all x2, waiting for transfers between devices, sent_to_all(): return lax.all_to_all(copies, axis, split_axis=0, concat_axis=0, tiled=True)  21.6 us
    all_to_all x2, starting transfers between devices, sent_to_all(): return lax.all_to_all(copies, axis, split_axis=0, concat_axis=0, tiled=True)  16.4 us
    all_to_all x2, starting transfers between devices, project_inputs(): lax.all_to_all(jnp.stack([weight] * lax.axis_size('fsdp')), 'fsdp', 0, 0)  10.3 us
    dot_general x2, matrix products, add_rows(): return jnp.dot(normed, segment, preferred_element_type=jnp.float32)  7.47 us
    sub x2, matrix products, attention_core(): exponent = jnp.exp(scores - row_max)  6.62 us
  transfers between devices with their start and end apart: 4, of which 4 were waited for; matrix products, arithmetic and copies ran while one was open for 6% of the time, Pallas kernels for 0%

profile of v1, /device:TPU:32, one launch (start us, length us, event | category | flops | bytes accessed | tf_op | source)
XLA Modules:
  0.0 276.1 jit_solution(40159349619842399)
XLA Ops:
  0.0 2.9 %stack.4 = bf16[16,64,1536]{2,1,0:T(8,128)(2,1)} broadcast(bf16[64,1536]{1,0:T(8,128)(2,1)} %param.9), dimensions={1,2} | broadcast | bytes 3342336 | tf_op jit(solution)/shard_map/stack | solution.py:61
  2.9 5.6 %all-to-all-start = ((bf16[16,64,1536]{2,1,0:T(8,128)(2,1)}), bf16[16,64,1536]{2,1,0:T(8,128)(2,1)}, u32[]{:S(2)}, u32[]{:S(2)}) async-start(bf16[16,64,1536]{2,1,0:T(8,128)(2,1)} %stack.4), calls=%async_computation | async-start | bytes 6291456 | tf_op jit(solution)/shard_map/all_to_all | solution.py:61
  9.2 38.5 %all-to-all-done = bf16[16,64,1536]{2,1,0:T(8,128)(2,1)} async-done(((bf16[16,64,1536]{2,1,0:T(8,128)(2,1)}), bf16[16,64,1536]{2,1,0:T(8,128)(2,1)}, u32[]{:S(2)}, u32[]{:S(2)}) %all-to-all-start) | async-done | bytes 3145760 | tf_op jit(solution)/shard_map/all_to_all | solution.py:61
  47.7 1.1 broadcast_in_dim.4
  48.8 8.6 %all-to-all-start.1 = ((bf16[16,32,1024]{2,1,0:T(8,128)(2,1)}), bf16[16,32,1024]{2,1,0:T(8,128)(2,1)}, u32[]{:S(2)}, u32[]{:S(2)}) async-start(bf16[16,32,1024]{2,1,0:T(8,128)(2,1)} %broadcast_in_dim.4), calls=%async_computation.1 | async-start | bytes 2097152 | tf_op jit(solution)/shard_map/all_to_all | solution.py:20
  57.5 3.8 %convolution_bitcast_fusion = bf16[2,256,1,1536]{3,1,0,2:T(8,128)(2,1)S(1)} fusion(bf16[1024,1536,1]{1,0,2:T(8,128)(2,1)} %bitcast.3, bf16[2,1,256,1024]{3,2,1,0:T(8,128)(2,1)S(1)} %copy-done, f32[1024]{0:T(1024)S(1)} %copy-done.7, f32[2,256]{1,0:T(2,128)S(1)} %add_rsqrt_fusion.1, f32[2,256]{1,0:T(2,128)S(1)} %broadcast_multiply_fusion.1), kind=kOutput, calls=%fused_computation.6 | convolution fusion | flops 1613234176 | bytes 5775360 | tf_op jit(solution)/shard_map/dot_general | solution.py:55
  62.0 3.4 %fusion.36 = (f32[2,8,256]{2,1,0:T(8,128)S(1)}, f32[2,8,256,256]{2,3,1,0:T(8,128)}) fusion(bf16[2,256,8,64]{1,3,2,0:T(8,128)(2,1)S(1)} %bitcast.67, bf16[2,256,8,64]{1,3,2,0:T(8,128)(2,1)S(1)} %bitcast.68), kind=kOutput, calls=%fused_computation.53 | convolution fusion | flops 137363712 | bytes 5259264 | tf_op jit(solution)/shard_map/sub | solution.py:44
  65.5 2.7 fusion.19
  68.2 0.5 copy.82
  68.8 5.2 %all-to-all-done.1 = bf16[16,32,1024]{2,1,0:T(8,128)(2,1)} async-done(((bf16[16,32,1024]{2,1,0:T(8,128)(2,1)}), bf16[16,32,1024]{2,1,0:T(8,128)(2,1)}, u32[]{:S(2)}, u32[]{:S(2)}) %all-to-all-start.1) | async-done | bytes 1048608 | tf_op jit(solution)/shard_map/all_to_all | solution.py:20
  74.0 2.0 fusion.10
  75.9 1.0 copy-done.1
  76.9 1.1 copy.83
  78.0 73.4 %all_to_all.38 = bf16[2,1,256,1024]{3,0,1,2:T(2,128)(2,1)S(1)} all-to-all(bf16[2,1,256,1024]{3,0,1,2:T(2,128)(2,1)S(1)} %copy.83), channel_id=1, replica_groups=mesh['fsdp'=16,'tm'=32] {'tm'}, dimensions={2} | all-to-all | bytes 2097152 | tf_op jit(solution)/shard_map/all_to_all | solution.py:91
  151.4 2.0 stack.5
  153.5 4.7 %all-to-all-start.3 = ((bf16[16,64,1536]{2,1,0:T(8,128)(2,1)}), bf16[16,64,1536]{2,1,0:T(8,128)(2,1)}, u32[]{:S(2)}, u32[]{:S(2)}) async-start(bf16[16,64,1536]{2,1,0:T(8,128)(2,1)} %stack.5), calls=%async_computation.3 | async-start | bytes 6291456 | tf_op jit(solution)/shard_map/all_to_all | solution.py:61
  158.1 0.9 convert_reduce_fusion
  159.0 1.8 fusion.7
  160.9 1.6 fusion.9
  162.5 34.6 %all-to-all-done.3 = bf16[16,64,1536]{2,1,0:T(8,128)(2,1)} async-done(((bf16[16,64,1536]{2,1,0:T(8,128)(2,1)}), bf16[16,64,1536]{2,1,0:T(8,128)(2,1)}, u32[]{:S(2)}, u32[]{:S(2)}) %all-to-all-start.3) | async-done | bytes 3145760 | tf_op jit(solution)/shard_map/all_to_all | solution.py:61
  197.1 3.7 %fusion.23 = bf16[2,32,8,1536]{3,2,1,0:T(8,128)(2,1)S(1)} fusion(bf16[1024,1536,1,1]{1,0,3,2:T(8,128)(2,1)} %bitcast.15, bf16[2,32,8,1024]{3,0,2,1:T(2,128)(2,1)S(1)} %bitcast.63), kind=kOutput, calls=%fused_computation.37 | convolution fusion | flops 1610612736 | bytes 5767168 | tf_op jit(solution)/shard_map/dot_general | solution.py:55
  200.9 0.5 reshape.180
  201.5 0.5 reshape.179
  202.0 1.5 reshape.178
  203.5 3.2 %fusion.37 = (f32[2,8,8,32]{3,2,1,0:T(8,128)S(1)}, f32[2,8,8,32,32]{3,4,2,1,0:T(8,128)}) fusion(bf16[2,32,8,8,64]{4,3,2,1,0:T(8,128)(2,1)S(1)} %reshape.180, bf16[2,32,8,8,64]{4,3,2,1,0:T(8,128)(2,1)S(1)} %reshape.179), kind=kOutput, calls=%fused_computation.54 | convolution fusion | flops 17170464 | bytes 1589248 | tf_op jit(solution)/shard_map/sub | solution.py:44
  206.7 2.9 %fusion.17 = bf16[2,32,8,8,64]{4,1,3,2,0:T(8,128)(2,1)S(1)} fusion(f32[2,8,8,32,32]{3,4,2,1,0:T(8,128)} %get-tuple-element.14, bf16[2,32,8,8,64]{4,3,2,1,0:T(8,128)(2,1)} %reshape.178, f32[2,8,8,32]{3,2,1,0:T(8,128)S(1)} %get-tuple-element.13), kind=kOutput, calls=%fused_computation.30 | convolution fusion | flops 17301504 | bytes 1589248 | tf_op jit(solution)/shard_map/bmhlk,bkmhe->blmhe/dot_general | solution.py:46
  210.0 0.6 reshape.188
  210.6 38.4 %all_to_all.39 = bf16[2,32,8,512]{3,2,0,1:T(8,128)(2,1)S(1)} all-to-all(bf16[2,32,8,512]{3,2,0,1:T(8,128)(2,1)S(1)} %reshape.188), channel_id=1, replica_groups=mesh['fsdp'=16,'tm'=32] {'tm'}, dimensions={1} | all-to-all | bytes 1048576 | tf_op jit(solution)/shard_map/all_to_all | solution.py:99
  249.0 1.1 broadcast_in_dim.5
  250.1 7.8 %all-to-all-start.5 = ((bf16[16,32,1024]{2,1,0:T(8,128)(2,1)}), bf16[16,32,1024]{2,1,0:T(8,128)(2,1)S(1)}, u32[]{:S(2)}, u32[]{:S(2)}) async-start(bf16[16,32,1024]{2,1,0:T(8,128)(2,1)} %broadcast_in_dim.5), calls=%async_computation.5 | async-start | bytes 2097152 | tf_op jit(solution)/shard_map/all_to_all | solution.py:20
  258.0 16.4 %all-to-all-done.5 = bf16[16,32,1024]{2,1,0:T(8,128)(2,1)S(1)} async-done(((bf16[16,32,1024]{2,1,0:T(8,128)(2,1)}), bf16[16,32,1024]{2,1,0:T(8,128)(2,1)S(1)}, u32[]{:S(2)}, u32[]{:S(2)}) %all-to-all-start.5) | async-done | bytes 1048608 | tf_op jit(solution)/shard_map/all_to_all | solution.py:20
  274.4 1.7 add_convert_fusion
  (29 shorter events, 2.1 us)
Async XLA Ops:
  2.9 5.6 %copy-start = (bf16[2,1,256,1024]{3,2,1,0:T(8,128)(2,1)S(1)}, bf16[2,1,256,1024]{3,2,1,0:T(8,128)(2,1)}, u32[]{:S(2)}) copy-start(bf16[2,1,256,1024]{3,2,1,0:T(8,128)(2,1)} %param.7) | copy-start | bytes 3145732
  2.9 44.8 %all-to-all-start = ((bf16[16,64,1536]{2,1,0:T(8,128)(2,1)}), bf16[16,64,1536]{2,1,0:T(8,128)(2,1)}, u32[]{:S(2)}, u32[]{:S(2)}) async-start(bf16[16,64,1536]{2,1,0:T(8,128)(2,1)} %stack.4), calls=%async_computation | async-start | bytes 6291456 | tf_op jit(solution)/shard_map/all_to_all | solution.py:61
  8.5 39.2 %copy-start.4 = (bf16[32,1024]{1,0:T(8,128)(2,1)S(1)}, bf16[32,1024]{1,0:T(8,128)(2,1)}, u32[]{:S(2)}) copy-start(bf16[32,1024]{1,0:T(8,128)(2,1)} %param.10) | copy-start | bytes 196612
  8.8 48.7 %copy-start.7 = (f32[1024]{0:T(1024)S(1)}, f32[1024]{0:T(1024)}, u32[]{:S(2)}) copy-start(f32[1024]{0:T(1024)} %param.8) | copy-start | bytes 12292
  48.8 25.2 %all-to-all-start.1 = ((bf16[16,32,1024]{2,1,0:T(8,128)(2,1)}), bf16[16,32,1024]{2,1,0:T(8,128)(2,1)}, u32[]{:S(2)}, u32[]{:S(2)}) async-start(bf16[16,32,1024]{2,1,0:T(8,128)(2,1)} %broadcast_in_dim.4), calls=%async_computation.1 | async-start | bytes 2097152 | tf_op jit(solution)/shard_map/all_to_all | solution.py:20
  75.9 1.0 copy-start.1
  76.9 74.5 %copy-start.3 = (bf16[64,1536]{1,0:T(8,128)(2,1)S(1)}, bf16[64,1536]{1,0:T(8,128)(2,1)}, u32[]{:S(2)}) copy-start(bf16[64,1536]{1,0:T(8,128)(2,1)} %param.12) | copy-start | bytes 589828
  153.5 43.6 %all-to-all-start.3 = ((bf16[16,64,1536]{2,1,0:T(8,128)(2,1)}), bf16[16,64,1536]{2,1,0:T(8,128)(2,1)}, u32[]{:S(2)}, u32[]{:S(2)}) async-start(bf16[16,64,1536]{2,1,0:T(8,128)(2,1)} %stack.5), calls=%async_computation.3 | async-start | bytes 6291456 | tf_op jit(solution)/shard_map/all_to_all | solution.py:61
  158.1 2.8 %copy-start.6 = (f32[1024]{0:T(1024)S(1)}, f32[1024]{0:T(1024)}, u32[]{:S(2)}) copy-start(f32[1024]{0:T(1024)} %param.11) | copy-start | bytes 12292
  209.6 39.4 %copy-start.5 = (bf16[32,1024]{1,0:T(8,128)(2,1)S(1)}, bf16[32,1024]{1,0:T(8,128)(2,1)}, u32[]{:S(2)}) copy-start(bf16[32,1024]{1,0:T(8,128)(2,1)} %param.13) | copy-start | bytes 196612
  249.0 25.4 %copy-start.2 = (bf16[512,1024]{1,0:T(8,128)(2,1)S(1)}, bf16[512,1024]{1,0:T(8,128)(2,1)}, u32[]{:S(2)}) copy-start(bf16[512,1024]{1,0:T(8,128)(2,1)} %copy-done.1) | copy-start | bytes 3145732
  250.1 24.3 %all-to-all-start.5 = ((bf16[16,32,1024]{2,1,0:T(8,128)(2,1)}), bf16[16,32,1024]{2,1,0:T(8,128)(2,1)S(1)}, u32[]{:S(2)}, u32[]{:S(2)}) async-start(bf16[16,32,1024]{2,1,0:T(8,128)(2,1)} %broadcast_in_dim.5), calls=%async_computation.5 | async-start | bytes 2097152 | tf_op jit(solution)/shard_map/all_to_all | solution.py:20
